TPU v7x, 32 devices: a whole 2x2x4 slice. The times are simulated.
32 devices in a mesh: seq: 8 (over z, y), tp: 4 (over x, core).
Axes of the slice: x: 2, y: 2, z: 4, core: 2. Of those that a mesh axis runs over, the one named last changes fastest.
Arguments:
- tokens: bfloat16 [8192, 1152], P('seq', 'tp'), may hold values from -6 to 6
- out_grad: bfloat16 [8192, 1152], P('seq', 'tp'), may hold values from -6 to 6
- route_mask: int32 [8192], P('seq'), may hold values from 0 to 1, as said below
- kept_counts: int32 [32], replicated, may hold values from 64 to 192, as said below
- labels: int32 [32], replicated, may hold values from 0 to 1000
- timesteps: int32 [32], replicated, may hold values from 0 to 999
- class_table: bfloat16 [1001, 1152], replicated, may hold values from -6 to 6
- ada_weight: bfloat16 [1152, 6, 1152], P(None, None, 'tp'), may hold values from -0.1875 to 0.1875
- ada_bias: bfloat16 [6, 1152], P(None, 'tp'), may hold values from -2 to 2
- qkv_weight: bfloat16 [1152, 3, 1152], P(None, None, 'tp'), may hold values from -0.1875 to 0.1875
- qv_bias: bfloat16 [2, 1152], P(None, 'tp'), may hold values from -2 to 2
- proj_weight: bfloat16 [1152, 1152], P('tp'), may hold values from -0.5 to 0.5
- proj_bias: bfloat16 [1152], P('tp'), may hold values from -2 to 2
- hidden_weight: bfloat16 [1152, 4608], P(None, 'tp'), may hold values from -0.1875 to 0.1875
- hidden_bias: bfloat16 [4608], P('tp'), may hold values from -2 to 2
- output_weight: bfloat16 [4608, 1152], P('tp'), may hold values from -0.09375 to 0.09375
- output_bias: bfloat16 [1152], P('tp'), may hold values from -2 to 2
Outputs:
- output: bfloat16 [8192, 1152], P('seq', 'tp')
- tokens_grad: bfloat16 [8192, 1152], P('seq', 'tp')
- class_grad: float32 [1001, 1152], P(None, 'seq')
- ada_weight_grad: float32 [1152, 6, 1152], P('seq', None, 'tp')
- ada_bias_grad: float32 [6, 1152], P(None, 'tp')
- qkv_weight_grad: float32 [1152, 3, 1152], P('seq', None, 'tp')
- qv_bias_grad: float32 [2, 1152], P(None, 'tp')
- proj_weight_grad: float32 [1152, 1152], P('tp', 'seq')
- proj_bias_grad: float32 [1152], P('tp')
- hidden_weight_grad: float32 [1152, 4608], P('seq', 'tp')
- hidden_bias_grad: float32 [4608], P('tp')
- output_weight_grad: float32 [4608, 1152], P('tp', 'seq')
- output_bias_grad: float32 [1152], P('tp')
Inputs may be any that keep to these rules, and one draw needn't show every extreme that they name: route_mask keeps exactly kept_counts[i] of the 256 tokens of image i. The kept tokens of all images number 512 * 8; the kept tokens of the first j * 4 images exceed j * 512 by 0 to 128 for every j, by exactly 128 for some j, and by 0 at the end. Every aligned block of 4 images has one image with 192 kept tokens. `route_mask`: consistent with kept_counts.
All inputs are finite; a program needn't handle non-finite values.
Results may differ from a plain program's by a relative error of at most 0.025.
The roundings to bfloat16 on the way count: a program that leaves them out, or rounds other values in their place, can miss the bound.
Values may be sent and summed in bfloat16 or wider, within the bound.
A program may use at most 192 MiB of HBM per device.

v0:
```python
import math
import jax
import jax.numpy as jnp
from jax import lax
from jax.sharding import PartitionSpec as P

HEAD_DIM = 72
IMG_DEV = 4
ROWS = 640
NORM_EPS = 1e-06
HIGHEST = lax.Precision.HIGHEST


def exact_dot(left_mat, right_mat):
    return jnp.dot(left_mat, right_mat, precision=HIGHEST, preferred_element_type=jnp.float32)


def time_embed(step_ids, model_width):
    half_width = model_width // 2
    frequency = jnp.exp(-math.log(10000.0) * jnp.arange(half_width, dtype=jnp.float32) / half_width)
    angles = step_ids.astype(jnp.float32)[:, None] * frequency[None, :]
    return jnp.concatenate([jnp.cos(angles), jnp.sin(angles)], axis=1)


def norm_rows(values):
    centered = values - jnp.mean(values, axis=1, keepdims=True)
    inverse = lax.rsqrt(jnp.mean(centered * centered, axis=1, keepdims=True) + NORM_EPS)
    return (centered * inverse, inverse)


def gelu_tanh(values):
    return jax.nn.gelu(values, approximate=True)


def local(
    tokens,
    out_grad,
    route_mask,
    kept_counts,
    labels,
    timesteps,
    class_table,
    ada_weight,
    ada_bias,
    qkv_weight,
    qv_bias,
    proj_weight,
    proj_bias,
    hidden_weight,
    hidden_bias,
    output_weight,
    output_bias,
):
    f32, bf16 = (jnp.float32, jnp.bfloat16)
    seq_index = lax.axis_index("seq")
    tp_index = lax.axis_index("tp")
    seq_size = lax.axis_size("seq")
    col_local = tokens.shape[1]
    model_width = class_table.shape[1]
    head_cols = qkv_weight.shape[2]
    heads_local = head_cols // HEAD_DIM
    slice_width = model_width // seq_size
    images = kept_counts.shape[0]
    scale_factor = HEAD_DIM ** (-0.5)
    col_start = tp_index * col_local
    first_image = seq_index * IMG_DEV
    own_counts = lax.dynamic_slice_in_dim(kept_counts, first_image, IMG_DEV)
    own_ends = jnp.cumsum(own_counts)
    rank = jnp.where(route_mask > 0, jnp.cumsum(route_mask) - 1, -1)
    row_ids = jnp.arange(ROWS, dtype=jnp.int32)
    place = (rank[None, :] == row_ids[:, None]).astype(bf16)
    row_image = jnp.sum((own_ends[None, :] <= row_ids[:, None]).astype(jnp.int32), axis=1)
    row_onehot = (row_image[:, None] == jnp.arange(IMG_DEV, dtype=jnp.int32)[None, :]).astype(f32)

    def whole_rows(part_rows):
        return lax.all_gather(part_rows, "tp", axis=1, tiled=True)

    def column_sum(part_rows):
        return lax.psum_scatter(
            part_rows.astype(bf16), "tp", scatter_dimension=1, tiled=True
        ).astype(f32)

    def own_cols(full_rows):
        return lax.dynamic_slice_in_dim(full_rows, col_start, col_local, 1)

    def reinsert(rows_new, initial):
        placed = jnp.einsum("rt,rc->tc", place, rows_new, preferred_element_type=f32).astype(bf16)
        return jnp.where(route_mask[:, None] > 0, placed, initial)

    label_hot = (
        labels[:, None] == jnp.arange(class_table.shape[0], dtype=jnp.int32)[None, :]
    ).astype(bf16)
    condition = jnp.dot(label_hot, class_table, preferred_element_type=f32) + time_embed(
        timesteps, model_width
    )
    cond_low = jax.nn.silu(condition).astype(bf16)
    cond_own = lax.dynamic_slice_in_dim(cond_low, first_image, IMG_DEV)
    mod_own = (
        jnp.einsum("wd,dcf->wcf", cond_own, ada_weight, preferred_element_type=f32)
        + ada_bias.astype(f32)[None]
    )
    mod_full = lax.all_gather(mod_own, "tp", axis=2, tiled=True)

    def row_full(stretch_id):
        return exact_dot(row_onehot, mod_full[:, stretch_id, :])

    def row_own(stretch_id):
        return exact_dot(row_onehot, mod_own[:, stretch_id, :])

    def input_grads(partial_rows, normed, inverse, scale):
        own_grad = column_sum(partial_rows)
        normed_own = own_cols(normed)
        scaled_grad = own_grad * (1.0 + own_cols(scale))
        mean_grad, mean_cross = lax.psum(
            (
                jnp.sum(scaled_grad, axis=1, keepdims=True) / model_width,
                jnp.sum(scaled_grad * normed_own, axis=1, keepdims=True) / model_width,
            ),
            "tp",
        )
        return (
            own_grad,
            own_grad * normed_own,
            inverse * (scaled_grad - mean_grad - normed_own * mean_cross),
        )

    picked = jnp.dot(place, jnp.concatenate([tokens, out_grad], axis=1), preferred_element_type=f32)
    rows_in = picked[:, :col_local].astype(bf16)
    grad_rows = picked[:, col_local:]
    gate_one = row_own(2)
    gate_two = row_own(5)
    mlp_grad = (grad_rows * gate_two).astype(bf16)
    full_in = whole_rows(rows_in).astype(f32)
    mlp_grad_full = whole_rows(mlp_grad)
    normed_one, inverse_one = norm_rows(full_in)
    scale_one = row_full(1)
    branch_one = (normed_one * (1.0 + scale_one) + row_full(0)).astype(bf16)
    qkv_bias = jnp.stack([qv_bias[0], jnp.zeros_like(qv_bias[0]), qv_bias[1]]).astype(f32)
    qkv_rows = (
        jnp.einsum("rd,dcf->rcf", branch_one, qkv_weight, preferred_element_type=f32)
        + qkv_bias[None]
    ).astype(bf16)
    query_all, key_all, value_all = (
        qkv_rows[:, part].reshape(ROWS, heads_local, HEAD_DIM) for part in range(3)
    )
    same_image = row_image[:, None] == row_image[None, :]
    raw = jnp.einsum("qhe,khe->hqk", query_all, key_all, preferred_element_type=f32) * scale_factor
    masked = jnp.where(same_image[None], raw, -1e30)
    top_score = jnp.max(masked, axis=2, keepdims=True)
    exp_scores = jnp.exp(masked - top_score)
    attn_probs = exp_scores / jnp.sum(exp_scores, axis=2, keepdims=True)
    probs_low = attn_probs.astype(bf16)
    attended = (
        jnp.einsum("hqk,khe->qhe", probs_low, value_all, preferred_element_type=f32)
        .reshape(ROWS, head_cols)
        .astype(bf16)
    )
    attn_out = column_sum(
        jnp.dot(attended, proj_weight, preferred_element_type=f32)
    ) + proj_bias.astype(f32)
    middle = rows_in.astype(f32) + gate_one * attn_out
    middle_full = whole_rows(middle.astype(bf16)).astype(f32)
    normed_two, inverse_two = norm_rows(middle_full)
    scale_two = row_full(4)
    branch_two = (normed_two * (1.0 + scale_two) + row_full(3)).astype(bf16)
    pre_act = jnp.dot(branch_two, hidden_weight, preferred_element_type=f32) + hidden_bias.astype(
        f32
    )
    act_low = gelu_tanh(pre_act).astype(bf16)
    mlp_out = column_sum(
        jnp.dot(act_low, output_weight, preferred_element_type=f32)
    ) + output_bias.astype(f32)
    final_rows = middle + gate_two * mlp_out
    output = reinsert(final_rows.astype(bf16), tokens)
    gate_two_rows = grad_rows * mlp_out
    output_bias_term = jnp.sum(mlp_grad, axis=0, dtype=f32)
    output_weight_term = jnp.einsum(
        "rf,rd->fd", act_low, mlp_grad_full, preferred_element_type=f32
    ).astype(bf16)
    act_grad = jnp.einsum("rd,fd->rf", mlp_grad_full, output_weight, preferred_element_type=f32)
    gelu_pull = jax.vjp(gelu_tanh, pre_act)[1]
    pre_grad = gelu_pull(act_grad)[0].astype(bf16)
    hidden_bias_term = jnp.sum(pre_grad, axis=0, dtype=f32)
    hidden_weight_term = jnp.einsum(
        "rd,rf->df", branch_two, pre_grad, preferred_element_type=f32
    ).astype(bf16)
    two_partial = jnp.einsum("rf,df->rd", pre_grad, hidden_weight, preferred_element_type=f32)
    shift_two_grad, scale_two_grad, two_norm_grad = input_grads(
        two_partial, normed_two, inverse_two, scale_two
    )
    middle_grad = grad_rows + two_norm_grad
    gate_one_rows = middle_grad * attn_out
    attn_grad = (middle_grad * gate_one).astype(bf16)
    proj_bias_term = jnp.sum(attn_grad, axis=0, dtype=f32)
    attn_grad_full = whole_rows(attn_grad)
    proj_weight_term = jnp.einsum(
        "rf,rd->fd", attended, attn_grad_full, preferred_element_type=f32
    ).astype(bf16)
    attended_grad = (
        jnp.einsum("rd,fd->rf", attn_grad_full, proj_weight, preferred_element_type=f32)
        .astype(bf16)
        .reshape(ROWS, heads_local, HEAD_DIM)
    )
    value_term = jnp.einsum("hqk,qhe->khe", probs_low, attended_grad, preferred_element_type=f32)
    prob_grad = jnp.einsum("qhe,khe->hqk", attended_grad, value_all, preferred_element_type=f32)
    row_dot = jnp.sum(attn_probs * prob_grad, axis=2, keepdims=True)
    score_grad = (attn_probs * (prob_grad - row_dot)).astype(bf16)
    query_term = (
        jnp.einsum("hqk,khe->qhe", score_grad, key_all, preferred_element_type=f32) * scale_factor
    )
    key_term = (
        jnp.einsum("hqk,qhe->khe", score_grad, query_all, preferred_element_type=f32) * scale_factor
    )
    qkv_grad = (
        jnp.stack([query_term, key_term, value_term], axis=1)
        .reshape(ROWS, 3, head_cols)
        .astype(bf16)
    )
    qkv_sums = jnp.sum(qkv_grad, axis=0, dtype=f32)
    qkv_weight_term = jnp.einsum(
        "rd,rcf->dcf", branch_one, qkv_grad, preferred_element_type=f32
    ).astype(bf16)
    one_partial = jnp.einsum("rcf,dcf->rd", qkv_grad, qkv_weight, preferred_element_type=f32)
    shift_one_grad, scale_one_grad, one_norm_grad = input_grads(
        one_partial, normed_one, inverse_one, scale_one
    )
    in_grad = middle_grad + one_norm_grad
    tokens_grad = reinsert(in_grad.astype(bf16), out_grad)
    per_row = jnp.concatenate(
        [
            shift_one_grad,
            scale_one_grad,
            gate_one_rows,
            shift_two_grad,
            scale_two_grad,
            gate_two_rows,
        ],
        axis=1,
    )
    mod_grad = jnp.einsum(
        "rw,rf->wf", row_onehot, per_row, precision=HIGHEST, preferred_element_type=f32
    )
    small = jnp.concatenate(
        [
            mod_grad.reshape(-1),
            qkv_sums[0],
            qkv_sums[2],
            proj_bias_term,
            hidden_bias_term,
            output_bias_term,
        ]
    )
    small_all = lax.all_gather(small, "seq", axis=0)
    mod_size = mod_grad.size
    mod_all = small_all[:, :mod_size].reshape(images, 6, col_local)
    bias_sums = jnp.sum(small_all[:, mod_size:], axis=0)
    ada_bias_grad = jnp.sum(mod_all, axis=0)
    qv_bias_grad = bias_sums[: 2 * col_local].reshape(2, col_local)
    at = 2 * col_local
    proj_bias_grad = bias_sums[at : at + col_local]
    at += col_local
    hidden_bias_grad = bias_sums[at : at + hidden_bias.shape[0]]
    at += hidden_bias.shape[0]
    output_bias_grad = bias_sums[at:]
    width_start = seq_index * slice_width
    cond_cols = lax.dynamic_slice_in_dim(condition, width_start, slice_width, 1)
    low_cols = lax.dynamic_slice_in_dim(cond_low, width_start, slice_width, 1)
    ada_weight_grad = jnp.einsum(
        "wd,wcf->dcf", low_cols.astype(f32), mod_all, precision=HIGHEST, preferred_element_type=f32
    )
    ada_rows = lax.dynamic_slice_in_dim(ada_weight, width_start, slice_width, 0)
    cond_grad = lax.psum(
        jnp.einsum(
            "wcf,dcf->wd",
            mod_all,
            ada_rows.astype(f32),
            precision=HIGHEST,
            preferred_element_type=f32,
        ),
        "tp",
    )
    silu_pull = jax.vjp(jax.nn.silu, cond_cols)[1]
    class_grad = jnp.einsum(
        "wc,wd->cd",
        label_hot.astype(f32),
        silu_pull(cond_grad)[0],
        precision=HIGHEST,
        preferred_element_type=f32,
    )
    qkv_weight_grad, proj_weight_grad, hidden_weight_grad, output_weight_grad = (
        lax.psum_scatter(qkv_weight_term, "seq", scatter_dimension=0, tiled=True).astype(f32),
        lax.psum_scatter(proj_weight_term, "seq", scatter_dimension=1, tiled=True).astype(f32),
        lax.psum_scatter(hidden_weight_term, "seq", scatter_dimension=0, tiled=True).astype(f32),
        lax.psum_scatter(output_weight_term, "seq", scatter_dimension=1, tiled=True).astype(f32),
    )
    return (
        output,
        tokens_grad,
        class_grad,
        ada_weight_grad,
        ada_bias_grad,
        qkv_weight_grad,
        qv_bias_grad,
        proj_weight_grad,
        proj_bias_grad,
        hidden_weight_grad,
        hidden_bias_grad,
        output_weight_grad,
        output_bias_grad,
    )


def solution(mesh):
    return jax.shard_map(
        local,
        mesh=mesh,
        in_specs=(
            P("seq", "tp"),
            P("seq", "tp"),
            P("seq"),
            P(),
            P(),
            P(),
            P(),
            P(None, None, "tp"),
            P(None, "tp"),
            P(None, None, "tp"),
            P(None, "tp"),
            P("tp", None),
            P("tp"),
            P(None, "tp"),
            P("tp"),
            P("tp", None),
            P("tp"),
        ),
        out_specs=(
            P("seq", "tp"),
            P("seq", "tp"),
            P(None, "seq"),
            P("seq", None, "tp"),
            P(None, "tp"),
            P("seq", None, "tp"),
            P(None, "tp"),
            P("tp", "seq"),
            P("tp"),
            P("seq", "tp"),
            P("tp"),
            P("tp", "seq"),
            P("tp"),
        ),
        check_vma=False,
    )
```

profile of v0, /device:TPU:0, one launch (start us, length us, event | category | flops | bytes accessed | tf_op | source)
XLA Modules:
  0.0 589.2 jit_solution(4795627765267242598)
XLA Ops:
  9.4 2.4 fusion.24
  14.4 2.9 multiply_convert_fusion.4
  17.3 3.5 convolution_add_fusion.4
  21.1 26.5 %all_gather.22 = f32[4,6,1152]{1,0,2:T(4,128)S(1)} all-gather(f32[4,6,288]{1,0,2:T(4,128)S(1)} %copy.102), channel_id=1, replica_groups=mesh['seq'=8,'tp'=4] {'tp'}, dimensions={2}, use_global_device_ids=true | all-gather | bytes 138240 | tf_op jit(solution)/shard_map/all_gather | solution.py:102
  47.6 6.0 %fusion.109 = (f32[4,1,1152]{1,0,2:T(4,128)}, f32[4,1,1152]{1,0,2:T(4,128)}, f32[4,1,1152]{1,0,2:T(4,128)}, f32[4,1,1152]{1,0,2:T(4,128)}) fusion(f32[4,6,1152]{1,0,2:T(4,128)S(1)} %all_gather.22), kind=kLoop, calls=%fused_computation.184 | loop fusion | bytes 147456 | tf_op jit(solution)/shard_map/slice | solution.py:105
  53.6 2.1 copy.105
  55.7 2.3 copy.103
  59.4 3.1 fusion.59
  66.1 3.9 fusion.21
  72.7 6.5 %fusion.113 = (f32[4,640]{1,0:T(4,128)S(1)}, f32[4,640,640]{1,2,0:T(8,128)}) fusion(pred[640,640]{0,1:T(8,128)(4,1)} %broadcast_compare_fusion, bf16[640,4,72]{0,2,1:T(8,128)(2,1)S(1)} %bitcast.99, bf16[640,4,72]{0,2,1:T(8,128)(2,1)S(1)} %bitcast.97), kind=kOutput, calls=%fused_computation.188 | convolution fusion | flops 242483840 | bytes 7710720 | tf_op jit(solution)/shard_map/sub | solution.py:150
  79.2 3.7 fusion.38
  83.7 2.2 convolution_convert_fusion.5
  85.9 2.7 convert_reduce_fusion.4
  88.8 25.1 %reduce-scatter.9.cloned.1.call-done = bf16[640,288]{0,1:T(8,128)(2,1)} async-done(((bf16[640,1152]{0,1:T(8,128)(2,1)}), bf16[640,288]{0,1:T(8,128)(2,1)}) %reduce-scatter.9.cloned.1.call-update) | async-done | bytes 368656 | tf_op jit(solution)/shard_map/reduce_scatter | solution.py:79
  113.9 2.9 fusion.78
  116.9 2.1 copy.111
  119.0 2.3 copy.109
  121.3 3.1 fusion.57
  124.4 10.8 %all-gather.10.cloned.1.call-done = bf16[640,1152]{0,1:T(8,128)(2,1)} async-done(((bf16[640,288]{0,1:T(8,128)(2,1)}), bf16[640,1152]{0,1:T(8,128)(2,1)}) %all-gather.10.cloned.1.call-update) | async-done | bytes 1474576 | tf_op jit(solution)/shard_map/all_gather | solution.py:76
  135.2 6.1 %fusion.115 = f32[640,1152]{0,1:T(8,128)} fusion(bf16[1152,1152]{1,0:T(8,128)(2,1)} %param.32, bf16[640,1152]{0,1:T(8,128)(2,1)} %all-gather.10.cloned.1.call-done), kind=kOutput, calls=%fused_computation.190 | convolution fusion | flops 1698693120 | bytes 7077888 | tf_op jit(solution)/shard_map/rd,fd->rf/dot_general | solution.py:180
  141.3 15.1 %all-gather.8.cloned.1.call-done = bf16[640,1152]{0,1:T(8,128)(2,1)} async-done(((bf16[640,288]{0,1:T(8,128)(2,1)}), bf16[640,1152]{0,1:T(8,128)(2,1)}) %all-gather.8.cloned.1.call-update) | async-done | bytes 1474576 | tf_op jit(solution)/shard_map/all_gather | solution.py:76
  160.0 3.9 fusion.11
  164.0 6.0 %convert_reduce_fusion.2 = (f32[1152]{0:T(1024)S(1)}, bf16[640,1152]{0,1:T(8,128)(2,1)S(1)}, f32[640,1152]{0,1:T(8,128)}) fusion(f32[640,1152]{0,1:T(8,128)S(1)} %copy-done.43, f32[1152]{0:T(1024)S(1)} %convert_element_type.178, bf16[640,1152]{0,1:T(8,128)(2,1)S(1)} %fusion.11, bf16[1152,1152]{1,0:T(8,128)(2,1)S(1)} %copy-done), kind=kOutput, calls=%fused_computation.42 | convolution fusion | flops 1715649408 | bytes 11510784 | tf_op jit(solution)/shard_map/dot_general | solution.py:166
  171.2 4.0 convolution_convert_fusion.3
  175.2 3.4 fusion.4
  178.6 24.3 %reduce-scatter.13.cloned.1.call-done = bf16[640,288]{0,1:T(8,128)(2,1)} async-done(((bf16[640,1152]{0,1:T(8,128)(2,1)}), bf16[640,288]{0,1:T(8,128)(2,1)}) %reduce-scatter.13.cloned.1.call-update) | async-done | bytes 368656 | tf_op jit(solution)/shard_map/reduce_scatter | solution.py:79
  204.3 5.9 all-reduce.1
  210.2 2.9 convert_reduce_fusion.5
  213.2 6.6 %convolution_convert_fusion.4 = bf16[640,1152]{0,1:T(8,128)(2,1)} fusion(bf16[1152,1152]{1,0:T(8,128)(2,1)} %param.32, f32[640,1152]{0,1:T(8,128)} %get-tuple-element.54), kind=kOutput, calls=%fused_computation.28 | convolution fusion | flops 1706065920 | bytes 7077888 | tf_op jit(solution)/shard_map/dot_general | solution.py:171
  219.8 5.4 convolution_convert_fusion.1
  225.3 5.8 convolution_convert_fusion
  231.4 2.1 all-gather.12.cloned.1.call-done
  233.5 2.4 convolution_convert_fusion.7
  237.9 4.1 multiply_reduce_fusion
  247.9 4.3 fusion.41
  252.2 3.2 fusion.9
  257.7 5.6 convolution_convert_fusion.2
  263.7 3.2 fusion.35
  267.2 71.5 %reduce-scatter.21.cloned.1.call-done = bf16[144,1152]{1,0:T(8,128)(2,1)} async-done(((bf16[1152,1152]{1,0:T(8,128)(2,1)}), bf16[144,1152]{1,0:T(8,128)(2,1)}) %reduce-scatter.21.cloned.1.call-update) | async-done | bytes 331792 | tf_op jit(solution)/shard_map/reduce_scatter | solution.py:293
  340.5 71.4 %reduce-scatter.23.cloned.1.call-done = bf16[1152,144]{0,1:T(8,128)(2,1)} async-done(((bf16[1152,1152]{0,1:T(8,128)(2,1)}), bf16[1152,144]{0,1:T(8,128)(2,1)}) %reduce-scatter.23.cloned.1.call-update) | async-done | bytes 331792 | tf_op jit(solution)/shard_map/reduce_scatter | solution.py:294
  413.8 62.3 %reduce-scatter.19.cloned.1.call-done = bf16[288,144]{0,1:T(8,128)(2,1)} async-done(((bf16[288,1152]{0,1:T(8,128)(2,1)}), bf16[288,144]{0,1:T(8,128)(2,1)}) %reduce-scatter.19.cloned.1.call-update) | async-done | bytes 82960 | tf_op jit(solution)/shard_map/reduce_scatter | solution.py:292
  477.7 27.7 %reduce-scatter.15.cloned.1.call-done = bf16[640,288]{0,1:T(8,128)(2,1)} async-done(((bf16[640,1152]{0,1:T(8,128)(2,1)}), bf16[640,288]{0,1:T(8,128)(2,1)}) %reduce-scatter.15.cloned.1.call-update) | async-done | bytes 368656 | tf_op jit(solution)/shard_map/reduce_scatter | solution.py:79
  509.6 2.3 fusion.64
  512.1 31.6 %all-gather = f32[73728]{0:T(1024)S(1)} all-gather(f32[9216]{0:T(1024)S(1)} %concatenate.21), channel_id=2, replica_groups=mesh['seq'=8,'tp'=4] {'seq'}, dimensions={0}, use_global_device_ids=true | all-gather | bytes 331776 | tf_op jit(solution)/shard_map/all_gather | solution.py:253
  548.1 11.1 %all-reduce = (f32[640]{0:T(1024)S(1)}, f32[640]{0:T(1024)S(1)}, f32[32,144]{1,0:T(8,128)S(1)}) all-reduce(f32[640]{0:T(1024)S(1)} %broadcast_multiply_fusion, f32[640]{0:T(1024)S(1)} %broadcast_multiply_fusion.1, f32[32,144]{1,0:T(8,128)S(1)} %convolution_bitcast_fusion.1), channel_id=1, replica_groups=mesh['seq'=8,'tp'=4] {'tp'}, use_global_device_ids=true, to_apply=%region_22.23 | all-reduce | flops 5888 | bytes 47104 | tf_op jit(solution)/shard_map/psum | solution.py:114
  559.9 2.1 fusion.73
  563.9 3.5 fusion.34
  567.3 12.9 %reduce-scatter.17.cloned.1.call-done = bf16[144,3,288]{2,0,1:T(8,128)(2,1)} async-done(((bf16[1152,3,288]{2,0,1:T(8,128)(2,1)}), bf16[144,3,288]{2,0,1:T(8,128)(2,1)}) %reduce-scatter.17.cloned.1.call-update) | async-done | bytes 248848 | tf_op jit(solution)/shard_map/reduce_scatter | solution.py:291
  (186 shorter events, 49.3 us)
Async XLA Ops:
  7.2 156.8 %copy-start = (bf16[1152,1152]{1,0:T(8,128)(2,1)S(1)}, bf16[1152,1152]{1,0:T(8,128)(2,1)}, u32[]{:S(2)}) copy-start(bf16[1152,1152]{1,0:T(8,128)(2,1)} %param.30) | copy-start | bytes 7962628
  7.2 55.3 %all-gather.6.cloned.1.call-start = ((), (), s32[]{:S(2)}) async-start(), calls=%async_computation.8 | async-start | bytes 1843200 | tf_op jit(solution)/shard_map/all_gather | solution.py:76
  9.3 4.4 copy-start.37
  9.3 4.7 copy-start.38
  9.3 4.7 copy-start.27
  9.3 5.1 copy-start.29
  13.7 100.2 %reduce-scatter.9.cloned.1.call-start = ((), (), s32[]{:S(2)}) async-start(), calls=%async_computation.9 | async-start | bytes 1843200 | tf_op jit(solution)/shard_map/reduce_scatter | solution.py:79
  53.6 4.6 copy-start.26
  62.5 3.6 copy-start.2
  66.1 3.9 copy-start.32
  72.7 6.5 %copy-start.16 = (bf16[640,1,288]{0,2,1:T(8,128)(2,1)}, bf16[640,1,288]{0,2,1:T(8,128)(2,1)S(1)}, u32[]{:S(2)}) copy-start(bf16[640,1,288]{0,2,1:T(8,128)(2,1)S(1)} %get-tuple-element.38) | copy-start | bytes 1105924
  72.7 6.5 %copy-start.17 = (bf16[640,1,288]{0,2,1:T(8,128)(2,1)}, bf16[640,1,288]{0,2,1:T(8,128)(2,1)S(1)}, u32[]{:S(2)}) copy-start(bf16[640,1,288]{0,2,1:T(8,128)(2,1)S(1)} %get-tuple-element.39) | copy-start | bytes 1105924
  79.2 4.5 copy-start.36
  83.7 5.1 copy-start.30
  85.9 31.0 %copy-start.28 = (bf16[1152]{0:T(1024)(128)(2,1)S(1)}, bf16[1152]{0:T(1024)(128)(2,1)}, u32[]{:S(2)}) copy-start(bf16[1152]{0:T(1024)(128)(2,1)} %param.31) | copy-start | bytes 6916
  85.9 49.3 %all-gather.10.cloned.1.call-start = ((), (), s32[]{:S(2)}) async-start(), calls=%async_computation.12 | async-start | bytes 1843200 | tf_op jit(solution)/shard_map/all_gather | solution.py:76
  88.7 67.7 %all-gather.8.cloned.1.call-start = ((), (), s32[]{:S(2)}) async-start(), calls=%async_computation.10 | async-start | bytes 1843200 | tf_op jit(solution)/shard_map/all_gather | solution.py:76
  116.8 86.1 %reduce-scatter.13.cloned.1.call-start = ((), (), s32[]{:S(2)}) async-start(), calls=%async_computation.13 | async-start | bytes 1843200 | tf_op jit(solution)/shard_map/reduce_scatter | solution.py:79
  156.4 3.6 copy-start.4
  160.0 4.0 copy-start.43
  164.0 6.0 %copy-start.12 = (bf16[640,1152]{0,1:T(8,128)(2,1)}, bf16[640,1152]{0,1:T(8,128)(2,1)S(1)}, u32[]{:S(2)}) copy-start(bf16[640,1152]{0,1:T(8,128)(2,1)S(1)} %fusion.11) | copy-start | bytes 4423684
  175.2 27.7 %copy-start.5 = (f32[640,1152]{0,1:T(8,128)S(1)}, f32[640,1152]{0,1:T(8,128)}, u32[]{:S(2)}) copy-start(f32[640,1152]{0,1:T(8,128)} %fusion.57) | copy-start | bytes 8847364
  175.2 58.3 %all-gather.12.cloned.1.call-start = ((), (), s32[]{:S(2)}) async-start(), calls=%async_computation.14 | async-start | bytes 1843200 | tf_op jit(solution)/shard_map/all_gather | solution.py:76
  213.1 50.6 %reduce-scatter.11.cloned.1.call-start = ((), (), s32[]{:S(2)}) async-start(), calls=%async_computation.11 | async-start | bytes 1843200 | tf_op jit(solution)/shard_map/reduce_scatter | solution.py:79
  213.2 6.7 %copy-start.13 = (bf16[640,1152]{0,1:T(8,128)(2,1)S(1)}, bf16[640,1152]{0,1:T(8,128)(2,1)}, u32[]{:S(2)}) copy-start(bf16[640,1152]{0,1:T(8,128)(2,1)} %copy-done.12) | copy-start | bytes 4423684
  219.8 5.6 copy-start.34
  219.8 118.9 %reduce-scatter.21.cloned.1.call-start = ((), (), s32[]{:S(2)}) async-start(), calls=%async_computation.18 | async-start | bytes 2985984 | tf_op jit(solution)/shard_map/reduce_scatter | solution.py:293
  225.3 186.7 %reduce-scatter.23.cloned.1.call-start = ((), (), s32[]{:S(2)}) async-start(), calls=%async_computation.19 | async-start | bytes 2985984 | tf_op jit(solution)/shard_map/reduce_scatter | solution.py:294
  231.2 4.7 copy-start.40
  231.2 244.9 %reduce-scatter.19.cloned.1.call-start = ((), (), s32[]{:S(2)}) async-start(), calls=%async_computation.17 | async-start | bytes 995328 | tf_op jit(solution)/shard_map/reduce_scatter | solution.py:292
  235.9 6.1 %copy-start.41 = (bf16[640,288]{0,1:T(8,128)(2,1)}, bf16[640,288]{0,1:T(8,128)(2,1)S(1)}, u32[]{:S(2)}) copy-start(bf16[640,288]{0,1:T(8,128)(2,1)S(1)} %convolution_convert_fusion.7) | copy-start | bytes 1105924
  237.9 4.3 slice-start
  237.9 5.1 slice-start.1
  246.0 259.4 %reduce-scatter.15.cloned.1.call-start = ((), (), s32[]{:S(2)}) async-start(), calls=%async_computation.15 | async-start | bytes 1843200 | tf_op jit(solution)/shard_map/reduce_scatter | solution.py:79
  247.8 4.4 copy-start.20
  247.8 4.4 copy-start.19
  247.8 4.4 copy-start.33
  252.2 3.3 copy-start.24
  252.2 3.5 copy-start.31
  252.2 3.5 copy-start.3
  255.5 324.8 %reduce-scatter.17.cloned.1.call-start = ((), (), s32[]{:S(2)}) async-start(), calls=%async_computation.16 | async-start | bytes 2985984 | tf_op jit(solution)/shard_map/reduce_scatter | solution.py:291
  257.7 6.0 %copy-start.7 = (f32[640,576]{0,1:T(8,128)S(1)}, f32[640,576]{0,1:T(8,128)}, u32[]{:S(2)}) copy-start(f32[640,576]{0,1:T(8,128)} %copy-done.6) | copy-start | bytes 4423684
  257.7 6.0 %copy-start.10 = (f32[640,288]{0,1:T(8,128)S(1)}, f32[640,288]{0,1:T(8,128)}, u32[]{:S(2)}) copy-start(f32[640,288]{0,1:T(8,128)} %get-tuple-element.52) | copy-start | bytes 2211844
  257.7 6.0 %copy-start.14 = (bf16[640,288]{0,1:T(8,128)(2,1)S(1)}, bf16[640,288]{0,1:T(8,128)(2,1)}, u32[]{:S(2)}) copy-start(bf16[640,288]{0,1:T(8,128)(2,1)} %reduce-scatter.9.cloned.1.call-done) | copy-start | bytes 1105924
  267.2 240.9 %copy-start.9 = (f32[640,288]{0,1:T(8,128)S(1)}, f32[640,288]{0,1:T(8,128)}, u32[]{:S(2)}) copy-start(f32[640,288]{0,1:T(8,128)} %get-tuple-element.30) | copy-start | bytes 2211844
  413.8 94.4 %copy-start.8 = (bf16[640,288]{0,1:T(8,128)(2,1)S(1)}, bf16[640,288]{0,1:T(8,128)(2,1)}, u32[]{:S(2)}) copy-start(bf16[640,288]{0,1:T(8,128)(2,1)} %reduce-scatter.13.cloned.1.call-done) | copy-start | bytes 1105924
  543.7 20.1 %copy-start.15 = (bf16[640,288]{0,1:T(8,128)(2,1)S(1)}, bf16[640,288]{0,1:T(8,128)(2,1)}, u32[]{:S(2)}) copy-start(bf16[640,288]{0,1:T(8,128)(2,1)} %reduce-scatter.15.cloned.1.call-done) | copy-start | bytes 1105924
  562.0 20.1 %copy-start.1 = (bf16[1152,1152]{1,0:T(8,128)(2,1)S(1)}, bf16[1152,1152]{1,0:T(8,128)(2,1)}, u32[]{:S(2)}) copy-start(bf16[1152,1152]{1,0:T(8,128)(2,1)} %param.30) | copy-start | bytes 7962628
  (11 other events, 18.8 us)
Sparse Core Ops, SparseCore 0:
  13.8 29.6 all-gather.5
  86.0 27.8 reduce-scatter.8
  116.1 19.0 all-gather.9
  137.3 19.0 all-gather.7
  175.3 27.5 reduce-scatter.12
  213.2 20.2 all-gather.11
  236.1 27.5 reduce-scatter.10
  267.8 70.8 reduce-scatter.20
  342.4 69.5 reduce-scatter.22
  416.2 59.8 reduce-scatter.18
  478.9 26.4 reduce-scatter.14
  508.9 71.3 reduce-scatter.16
where the time goes:
time: 595 us; the launch traced here: 589 us
  waiting for transfers between devices  324 us (54%)
  matrix products  117 us (20%)
  blocking collectives  75 us (13%)
  other arithmetic  33.7 us (6%)
  local copies, waits for them, and re-layouts  23.8 us (4%)
  between operations  15.1 us (3%)
    reduce_scatter x4, waiting for transfers between devices, column_sum(): lax.psum_scatter(part_rows.astype(bf16), 'tp', scatter_dimension=1, tiled...  77.5 us
    reduce_scatter x1, waiting for transfers between devices, local(): lax.psum_scatter(hidden_weight_term, 'seq', scatter_dimension=0, tiled=True)  71.5 us
    reduce_scatter x1, waiting for transfers between devices, local(): lax.psum_scatter(output_weight_term, 'seq', scatter_dimension=1, tiled=True)  71.4 us
    reduce_scatter x1, waiting for transfers between devices, local(): lax.psum_scatter(proj_weight_term, 'seq', scatter_dimension=1, tiled=True)  62.3 us
    all_gather x1, blocking collectives, local(): small_all = lax.all_gather(small, 'seq', axis=0)  31.6 us
    all_gather x4, waiting for transfers between devices, whole_rows(): return lax.all_gather(part_rows, 'tp', axis=1, tiled=True)  28 us
    all_gather x1, blocking collectives, local(): mod_full = lax.all_gather(mod_own, 'tp', axis=2, tiled=True)  26.5 us
    dot_general x6, matrix products, exact_dot(): jnp.dot(left_mat, right_mat, precision=HIGHEST, preferred_element_type=jn...  19.7 us
  transfers between devices with their start and end apart: 12, of which 11 were waited for; matrix products, arithmetic and copies ran while one was open for 20% of the time, Pallas kernels for 0%

commit v1 on v0

--- a/solution.py
+++ b/solution.py
@@ -99,7 +99,19 @@
         jnp.einsum("wd,dcf->wcf", cond_own, ada_weight, preferred_element_type=f32)
         + ada_bias.astype(f32)[None]
     )
-    mod_full = lax.all_gather(mod_own, "tp", axis=2, tiled=True)
+    how_many = lax.axis_size("tp")
+    all_blocks = [mod_own]
+    ii = 0
+    while ii < how_many - 1:
+        all_blocks.append(
+            lax.ppermute(all_blocks[-1], "tp", [(j, (j + 1) % how_many) for j in range(how_many)])
+        )
+        ii = ii + 1
+    mod_full = jnp.roll(
+        jnp.concatenate(all_blocks[::-1], axis=2),
+        shift=(lax.axis_index("tp") + 1) * mod_own.shape[2],
+        axis=2,
+    )
 
     def row_full(stretch_id):
         return exact_dot(row_onehot, mod_full[:, stretch_id, :])

time: 595 us -> 570 us (0.958)
  blocking collectives: 75 us -> 48.2 us
  waiting for transfers between devices: 324 us -> 339 us
  local copies, waits for them, and re-layouts: 23.8 us -> 8.91 us
    all_gather x1 -> x0, blocking collectives: 26.5 us -> none  [local(): mod_full = lax.all_gather(mod_own, 'tp', axis=2, tiled=True)]
    slice x6 -> x1, local copies, waits for them, and re-layouts: 15 us -> 0.07 us  [the longest x5 14.9 us: row_full(): return exact_dot(row_onehot, mod_full[:, stretch_id, :])]
    ppermute x0 -> x3, waiting for transfers between devices: none -> 9.11 us  [local(): lax.ppermute(all_blocks[-1], 'tp', [(j, (j + 1) % how_many) for j in rang...]
  transfers between devices with their start and end apart: 12 -> 15, of which waited for: 11 -> 15; matrix products, arithmetic and copies ran while one was open for 20% -> 18% of each run, Pallas kernels for 0% -> 0%
where the time goes in v1:
time: 570 us; the launch traced here: 566 us
  waiting for transfers between devices  339 us (59%)
  matrix products  118 us (21%)
  blocking collectives  48.2 us (8%)
  other arithmetic  33.7 us (6%)
  between operations  15.1 us (3%)
  local copies, waits for them, and re-layouts  8.91 us (2%)
    reduce_scatter x4, waiting for transfers between devices, column_sum(): lax.psum_scatter(part_rows.astype(bf16), 'tp', scatter_dimension=1, tiled...  79.6 us
    reduce_scatter x1, waiting for transfers between devices, local(): lax.psum_scatter(output_weight_term, 'seq', scatter_dimension=1, tiled=True)  71.5 us
    reduce_scatter x1, waiting for transfers between devices, local(): lax.psum_scatter(hidden_weight_term, 'seq', scatter_dimension=0, tiled=True)  71.2 us
    reduce_scatter x1, waiting for transfers between devices, local(): lax.psum_scatter(proj_weight_term, 'seq', scatter_dimension=1, tiled=True)  62.6 us
    all_gather x1, blocking collectives, local(): small_all = lax.all_gather(small, 'seq', axis=0)  31.7 us
    all_gather x4, waiting for transfers between devices, whole_rows(): return lax.all_gather(part_rows, 'tp', axis=1, tiled=True)  31.6 us
    dot_general x6, matrix products, exact_dot(): jnp.dot(left_mat, right_mat, precision=HIGHEST, preferred_element_type=jn...  20.8 us
    psum x2, blocking collectives, input_grads(): lax.psum((jnp.sum(scaled_grad, axis=1, keepdims=True) / model_width, jnp....  16.5 us
  transfers between devices with their start and end apart: 15, of which 15 were waited for; matrix products, arithmetic and copies ran while one was open for 18% of the time, Pallas kernels for 0%

profile of v1, /device:TPU:0, one launch (start us, length us, event | category | flops | bytes accessed | tf_op | source)
XLA Modules:
  0.0 565.6 jit_solution(3628967667367721034)
XLA Ops:
  9.3 2.4 fusion.24
  14.2 2.9 multiply_convert_fusion.4
  17.1 3.5 convolution_add_fusion.4
  22.4 2.2 collective-permute-done
  25.1 3.4 collective-permute-done.1
  29.3 3.5 collective-permute-done.2
  33.1 3.2 fusion.59
  40.1 4.0 fusion.21
  46.8 6.5 %fusion.112 = (f32[4,640]{1,0:T(4,128)S(1)}, f32[4,640,640]{1,2,0:T(8,128)}) fusion(pred[640,640]{0,1:T(8,128)(4,1)} %broadcast_compare_fusion, bf16[640,4,72]{0,2,1:T(8,128)(2,1)S(1)} %bitcast.99, bf16[640,4,72]{0,2,1:T(8,128)(2,1)S(1)} %bitcast.97), kind=kOutput, calls=%fused_computation.191 | convolution fusion | flops 242483840 | bytes 7710720 | tf_op jit(solution)/shard_map/sub | solution.py:162
  53.3 3.7 fusion.38
  57.8 2.2 convolution_convert_fusion.5
  60.0 2.7 convert_reduce_fusion.4
  62.9 27.2 %reduce-scatter.9.cloned.1.call-done = bf16[640,288]{0,1:T(8,128)(2,1)} async-done(((bf16[640,1152]{0,1:T(8,128)(2,1)}), bf16[640,288]{0,1:T(8,128)(2,1)}) %reduce-scatter.9.cloned.1.call-update) | async-done | bytes 368656 | tf_op jit(solution)/shard_map/reduce_scatter | solution.py:79
  90.1 2.9 fusion.78
  93.3 3.9 fusion.57
  97.2 14.3 %all-gather.10.cloned.1.call-done = bf16[640,1152]{0,1:T(8,128)(2,1)} async-done(((bf16[640,288]{0,1:T(8,128)(2,1)}), bf16[640,1152]{0,1:T(8,128)(2,1)}) %all-gather.10.cloned.1.call-update) | async-done | bytes 1474576 | tf_op jit(solution)/shard_map/all_gather | solution.py:76
  111.4 6.1 %fusion.114 = f32[640,1152]{0,1:T(8,128)} fusion(bf16[1152,1152]{1,0:T(8,128)(2,1)} %param.32, bf16[640,1152]{0,1:T(8,128)(2,1)} %all-gather.10.cloned.1.call-done), kind=kOutput, calls=%fused_computation.193 | convolution fusion | flops 1698693120 | bytes 7077888 | tf_op jit(solution)/shard_map/rd,fd->rf/dot_general | solution.py:192
  117.6 15.1 %all-gather.8.cloned.1.call-done = bf16[640,1152]{0,1:T(8,128)(2,1)} async-done(((bf16[640,288]{0,1:T(8,128)(2,1)}), bf16[640,1152]{0,1:T(8,128)(2,1)}) %all-gather.8.cloned.1.call-update) | async-done | bytes 1474576 | tf_op jit(solution)/shard_map/all_gather | solution.py:76
  136.3 4.0 fusion.11
  140.4 6.0 %convert_reduce_fusion.2 = (f32[1152]{0:T(1024)S(1)}, bf16[640,1152]{0,1:T(8,128)(2,1)S(1)}, f32[640,1152]{0,1:T(8,128)}) fusion(f32[640,1152]{0,1:T(8,128)S(1)} %copy-done.44, f32[1152]{0:T(1024)S(1)} %convert_element_type.178, bf16[640,1152]{0,1:T(8,128)(2,1)S(1)} %fusion.11, bf16[1152,1152]{1,0:T(8,128)(2,1)S(1)} %copy-done), kind=kOutput, calls=%fused_computation.42 | convolution fusion | flops 1715649408 | bytes 11510784 | tf_op jit(solution)/shard_map/dot_general | solution.py:178
  147.5 3.9 convolution_convert_fusion.3
  151.5 3.4 fusion.4
  154.9 24.3 %reduce-scatter.13.cloned.1.call-done = bf16[640,288]{0,1:T(8,128)(2,1)} async-done(((bf16[640,1152]{0,1:T(8,128)(2,1)}), bf16[640,288]{0,1:T(8,128)(2,1)}) %reduce-scatter.13.cloned.1.call-update) | async-done | bytes 368656 | tf_op jit(solution)/shard_map/reduce_scatter | solution.py:79
  180.6 5.9 %all-reduce.1 = (f32[640]{0:T(1024)S(1)}, f32[640]{0:T(1024)S(1)}) all-reduce(f32[640]{0:T(1024)S(1)} %get-tuple-element.53, f32[640]{0:T(1024)S(1)} %get-tuple-element.54), channel_id=1, replica_groups=mesh['seq'=8,'tp'=4] {'tp'}, use_global_device_ids=true, to_apply=%region_16.17 | all-reduce | flops 1280 | bytes 10240 | tf_op jit(solution)/shard_map/psum | solution.py:126
  186.5 2.9 convert_reduce_fusion.5
  189.5 6.5 %convolution_convert_fusion.4 = bf16[640,1152]{0,1:T(8,128)(2,1)} fusion(bf16[1152,1152]{1,0:T(8,128)(2,1)} %param.32, f32[640,1152]{0,1:T(8,128)} %get-tuple-element.50), kind=kOutput, calls=%fused_computation.28 | convolution fusion | flops 1706065920 | bytes 7077888 | tf_op jit(solution)/shard_map/dot_general | solution.py:183
  196.1 5.4 convolution_convert_fusion.1
  201.6 5.8 %convolution_convert_fusion = bf16[1152,1152]{0,1:T(8,128)(2,1)} fusion(bf16[640,1152]{0,1:T(8,128)(2,1)S(1)} %copy-done.35, f32[640,1152]{0,1:T(8,128)} %get-tuple-element.50), kind=kOutput, calls=%fused_computation.1 | convolution fusion | flops 1706655744 | bytes 7077888 | tf_op jit(solution)/shard_map/rf,rd->fd/dot_general | solution.py:189
  207.7 2.1 all-gather.12.cloned.1.call-done
  209.8 2.4 convolution_convert_fusion.7
  212.3 1.9 convolution_convert_fusion.6
  214.2 4.1 multiply_reduce_fusion
  220.3 2.0 fusion.37
  224.2 4.3 fusion.41
  228.5 3.2 fusion.9
  234.0 5.5 convolution_convert_fusion.2
  240.0 3.2 fusion.35
  243.5 71.2 %reduce-scatter.21.cloned.1.call-done = bf16[144,1152]{1,0:T(8,128)(2,1)} async-done(((bf16[1152,1152]{1,0:T(8,128)(2,1)}), bf16[144,1152]{1,0:T(8,128)(2,1)}) %reduce-scatter.21.cloned.1.call-update) | async-done | bytes 331792 | tf_op jit(solution)/shard_map/reduce_scatter | solution.py:305
  316.5 71.5 %reduce-scatter.23.cloned.1.call-done = bf16[1152,144]{0,1:T(8,128)(2,1)} async-done(((bf16[1152,1152]{0,1:T(8,128)(2,1)}), bf16[1152,144]{0,1:T(8,128)(2,1)}) %reduce-scatter.23.cloned.1.call-update) | async-done | bytes 331792 | tf_op jit(solution)/shard_map/reduce_scatter | solution.py:306
  389.9 62.6 %reduce-scatter.19.cloned.1.call-done = bf16[288,144]{0,1:T(8,128)(2,1)} async-done(((bf16[288,1152]{0,1:T(8,128)(2,1)}), bf16[288,144]{0,1:T(8,128)(2,1)}) %reduce-scatter.19.cloned.1.call-update) | async-done | bytes 82960 | tf_op jit(solution)/shard_map/reduce_scatter | solution.py:304
  454.1 27.7 %reduce-scatter.15.cloned.1.call-done = bf16[640,288]{0,1:T(8,128)(2,1)} async-done(((bf16[640,1152]{0,1:T(8,128)(2,1)}), bf16[640,288]{0,1:T(8,128)(2,1)}) %reduce-scatter.15.cloned.1.call-update) | async-done | bytes 368656 | tf_op jit(solution)/shard_map/reduce_scatter | solution.py:79
  486.1 2.3 fusion.64
  488.6 31.7 %all-gather = f32[73728]{0:T(1024)S(1)} all-gather(f32[9216]{0:T(1024)S(1)} %concatenate.28), channel_id=2, replica_groups=mesh['seq'=8,'tp'=4] {'seq'}, dimensions={0}, use_global_device_ids=true | all-gather | bytes 331776 | tf_op jit(solution)/shard_map/all_gather | solution.py:265
  522.6 2.0 convolution_bitcast_fusion.1
  524.7 10.6 %all-reduce = (f32[640]{0:T(1024)S(1)}, f32[640]{0:T(1024)S(1)}, f32[32,144]{1,0:T(8,128)S(1)}) all-reduce(f32[640]{0:T(1024)S(1)} %broadcast_multiply_fusion, f32[640]{0:T(1024)S(1)} %broadcast_multiply_fusion.1, f32[32,144]{1,0:T(8,128)S(1)} %convolution_bitcast_fusion.1), channel_id=1, replica_groups=mesh['seq'=8,'tp'=4] {'tp'}, use_global_device_ids=true, to_apply=%region_22.23 | all-reduce | flops 5888 | bytes 47104 | tf_op jit(solution)/shard_map/psum | solution.py:126
  536.0 2.1 fusion.73
  540.0 3.6 fusion.34
  543.5 13.1 %reduce-scatter.17.cloned.1.call-done = bf16[144,3,288]{2,0,1:T(8,128)(2,1)} async-done(((bf16[1152,3,288]{2,0,1:T(8,128)(2,1)}), bf16[144,3,288]{2,0,1:T(8,128)(2,1)}) %reduce-scatter.17.cloned.1.call-update) | async-done | bytes 248848 | tf_op jit(solution)/shard_map/reduce_scatter | solution.py:303
  (188 shorter events, 45.3 us)
Async XLA Ops:
  7.2 133.1 %copy-start = (bf16[1152,1152]{1,0:T(8,128)(2,1)S(1)}, bf16[1152,1152]{1,0:T(8,128)(2,1)}, u32[]{:S(2)}) copy-start(bf16[1152,1152]{1,0:T(8,128)(2,1)} %param.30) | copy-start | bytes 7962628
  7.2 29.2 %all-gather.6.cloned.1.call-start = ((), (), s32[]{:S(2)}) async-start(), calls=%async_computation.8 | async-start | bytes 1843200 | tf_op jit(solution)/shard_map/all_gather | solution.py:76
  9.3 4.4 copy-start.38
  9.3 4.4 copy-start.28
  9.3 4.8 copy-start.30
  13.7 76.4 %reduce-scatter.9.cloned.1.call-start = ((), (), s32[]{:S(2)}) async-start(), calls=%async_computation.9 | async-start | bytes 1843200 | tf_op jit(solution)/shard_map/reduce_scatter | solution.py:79
  14.2 6.8 %copy-start.39 = (s32[32]{0:T(128)S(1)}, s32[32]{0:T(128)}, u32[]{:S(2)}) copy-start(s32[32]{0:T(128)} %param.20) | copy-start | bytes 388
  14.2 10.8 %copy-start.27 = (bf16[2,288]{1,0:T(2,128)(2,1)S(1)}, bf16[2,288]{1,0:T(2,128)(2,1)}, u32[]{:S(2)}) copy-start(bf16[2,288]{1,0:T(2,128)(2,1)} %param.27) | copy-start | bytes 3460
  20.5 4.0 collective-permute-start
  24.6 3.9 collective-permute-start.1
  28.5 4.3 collective-permute-start.2
  33.1 6.9 %copy-start.22 = (f32[4,6,2304]{2,0,1:T(4,128)}, f32[4,6,2304]{2,0,1:T(4,128)S(1)}, u32[]{:S(2)}) copy-start(f32[4,6,2304]{2,0,1:T(4,128)S(1)} %concatenate.26) | copy-start | bytes 663556
  36.4 3.6 copy-start.2
  40.1 4.0 copy-start.33
  46.8 6.5 %copy-start.16 = (bf16[640,1,288]{0,2,1:T(8,128)(2,1)}, bf16[640,1,288]{0,2,1:T(8,128)(2,1)S(1)}, u32[]{:S(2)}) copy-start(bf16[640,1,288]{0,2,1:T(8,128)(2,1)S(1)} %get-tuple-element.34) | copy-start | bytes 1105924
  46.8 6.5 %copy-start.17 = (bf16[640,1,288]{0,2,1:T(8,128)(2,1)}, bf16[640,1,288]{0,2,1:T(8,128)(2,1)S(1)}, u32[]{:S(2)}) copy-start(bf16[640,1,288]{0,2,1:T(8,128)(2,1)S(1)} %get-tuple-element.35) | copy-start | bytes 1105924
  53.3 4.5 copy-start.37
  57.8 5.1 copy-start.31
  60.0 33.3 %copy-start.29 = (bf16[1152]{0:T(1024)(128)(2,1)S(1)}, bf16[1152]{0:T(1024)(128)(2,1)}, u32[]{:S(2)}) copy-start(bf16[1152]{0:T(1024)(128)(2,1)} %param.31) | copy-start | bytes 6916
  60.0 51.5 %all-gather.10.cloned.1.call-start = ((), (), s32[]{:S(2)}) async-start(), calls=%async_computation.12 | async-start | bytes 1843200 | tf_op jit(solution)/shard_map/all_gather | solution.py:76
  62.8 69.9 %all-gather.8.cloned.1.call-start = ((), (), s32[]{:S(2)}) async-start(), calls=%async_computation.10 | async-start | bytes 1843200 | tf_op jit(solution)/shard_map/all_gather | solution.py:76
  93.0 86.2 %reduce-scatter.13.cloned.1.call-start = ((), (), s32[]{:S(2)}) async-start(), calls=%async_computation.13 | async-start | bytes 1843200 | tf_op jit(solution)/shard_map/reduce_scatter | solution.py:79
  136.3 4.1 copy-start.44
  140.3 6.1 %copy-start.12 = (bf16[640,1152]{0,1:T(8,128)(2,1)}, bf16[640,1152]{0,1:T(8,128)(2,1)S(1)}, u32[]{:S(2)}) copy-start(bf16[640,1152]{0,1:T(8,128)(2,1)S(1)} %fusion.11) | copy-start | bytes 4423684
  151.5 27.7 %copy-start.5 = (f32[640,1152]{0,1:T(8,128)S(1)}, f32[640,1152]{0,1:T(8,128)}, u32[]{:S(2)}) copy-start(f32[640,1152]{0,1:T(8,128)} %fusion.57) | copy-start | bytes 8847364
  151.5 58.3 %all-gather.12.cloned.1.call-start = ((), (), s32[]{:S(2)}) async-start(), calls=%async_computation.14 | async-start | bytes 1843200 | tf_op jit(solution)/shard_map/all_gather | solution.py:76
  189.4 50.6 %reduce-scatter.11.cloned.1.call-start = ((), (), s32[]{:S(2)}) async-start(), calls=%async_computation.11 | async-start | bytes 1843200 | tf_op jit(solution)/shard_map/reduce_scatter | solution.py:79
  189.5 6.6 %copy-start.13 = (bf16[640,1152]{0,1:T(8,128)(2,1)S(1)}, bf16[640,1152]{0,1:T(8,128)(2,1)}, u32[]{:S(2)}) copy-start(bf16[640,1152]{0,1:T(8,128)(2,1)} %copy-done.12) | copy-start | bytes 4423684
  196.0 5.6 copy-start.35
  196.0 118.6 %reduce-scatter.21.cloned.1.call-start = ((), (), s32[]{:S(2)}) async-start(), calls=%async_computation.18 | async-start | bytes 2985984 | tf_op jit(solution)/shard_map/reduce_scatter | solution.py:305
  201.5 186.5 %reduce-scatter.23.cloned.1.call-start = ((), (), s32[]{:S(2)}) async-start(), calls=%async_computation.19 | async-start | bytes 2985984 | tf_op jit(solution)/shard_map/reduce_scatter | solution.py:306
  207.4 4.8 copy-start.41
  207.4 245.1 %reduce-scatter.19.cloned.1.call-start = ((), (), s32[]{:S(2)}) async-start(), calls=%async_computation.17 | async-start | bytes 995328 | tf_op jit(solution)/shard_map/reduce_scatter | solution.py:304
  212.2 6.1 %copy-start.42 = (bf16[640,288]{0,1:T(8,128)(2,1)}, bf16[640,288]{0,1:T(8,128)(2,1)S(1)}, u32[]{:S(2)}) copy-start(bf16[640,288]{0,1:T(8,128)(2,1)S(1)} %convolution_convert_fusion.7) | copy-start | bytes 1105924
  214.2 4.3 slice-start
  214.2 5.1 slice-start.1
  222.3 259.5 %reduce-scatter.15.cloned.1.call-start = ((), (), s32[]{:S(2)}) async-start(), calls=%async_computation.15 | async-start | bytes 1843200 | tf_op jit(solution)/shard_map/reduce_scatter | solution.py:79
  224.1 4.4 copy-start.20
  224.1 4.4 copy-start.19
  224.1 4.4 copy-start.34
  231.8 324.9 %reduce-scatter.17.cloned.1.call-start = ((), (), s32[]{:S(2)}) async-start(), calls=%async_computation.16 | async-start | bytes 2985984 | tf_op jit(solution)/shard_map/reduce_scatter | solution.py:303
  233.9 6.0 %copy-start.7 = (f32[640,576]{0,1:T(8,128)S(1)}, f32[640,576]{0,1:T(8,128)}, u32[]{:S(2)}) copy-start(f32[640,576]{0,1:T(8,128)} %copy-done.6) | copy-start | bytes 4423684
  233.9 6.0 %copy-start.10 = (f32[640,288]{0,1:T(8,128)S(1)}, f32[640,288]{0,1:T(8,128)}, u32[]{:S(2)}) copy-start(f32[640,288]{0,1:T(8,128)} %get-tuple-element.48) | copy-start | bytes 2211844
  233.9 6.0 %copy-start.14 = (bf16[640,288]{0,1:T(8,128)(2,1)S(1)}, bf16[640,288]{0,1:T(8,128)(2,1)}, u32[]{:S(2)}) copy-start(bf16[640,288]{0,1:T(8,128)(2,1)} %reduce-scatter.9.cloned.1.call-done) | copy-start | bytes 1105924
  243.5 241.0 %copy-start.9 = (f32[640,288]{0,1:T(8,128)S(1)}, f32[640,288]{0,1:T(8,128)}, u32[]{:S(2)}) copy-start(f32[640,288]{0,1:T(8,128)} %get-tuple-element.30) | copy-start | bytes 2211844
  389.9 94.8 %copy-start.8 = (bf16[640,288]{0,1:T(8,128)(2,1)S(1)}, bf16[640,288]{0,1:T(8,128)(2,1)}, u32[]{:S(2)}) copy-start(bf16[640,288]{0,1:T(8,128)(2,1)} %reduce-scatter.13.cloned.1.call-done) | copy-start | bytes 1105924
  520.3 19.7 %copy-start.15 = (bf16[640,288]{0,1:T(8,128)(2,1)S(1)}, bf16[640,288]{0,1:T(8,128)(2,1)}, u32[]{:S(2)}) copy-start(bf16[640,288]{0,1:T(8,128)(2,1)} %reduce-scatter.15.cloned.1.call-done) | copy-start | bytes 1105924
  538.1 20.4 %copy-start.1 = (bf16[1152,1152]{1,0:T(8,128)(2,1)S(1)}, bf16[1152,1152]{1,0:T(8,128)(2,1)}, u32[]{:S(2)}) copy-start(bf16[1152,1152]{1,0:T(8,128)(2,1)} %param.30) | copy-start | bytes 7962628
  (15 other events, 32.7 us)
Sparse Core Ops, SparseCore 0:
  13.8 22.5 all-gather.5
  60.1 29.9 reduce-scatter.8
  92.3 19.1 all-gather.9
  113.5 19.0 all-gather.7
  151.6 27.5 reduce-scatter.12
  189.5 20.2 all-gather.11
  212.4 27.5 reduce-scatter.10
  244.1 70.5 reduce-scatter.20
  318.3 69.6 reduce-scatter.22
  392.3 60.2 reduce-scatter.18
  455.3 26.4 reduce-scatter.14
  485.3 71.2 reduce-scatter.16
